TPU v7x, 32 devices: a whole 2x2x4 slice. The times are simulated.
32 devices in a mesh: groups: 2 (over y), row: 4 (over z), col: 4 (over x, core).
Axes of the slice: x: 2, y: 2, z: 4, core: 2. Of those that a mesh axis runs over, the one named last changes fastest.
Arguments:
- factor_blocks: bfloat16 [20, 4096, 4096], P('groups', 'row', 'col'), parts along dimension 0, may hold values from -0.0390625 to 0.0390625
- inverse_blocks: bfloat16 [10, 4096, 4096], P('groups', 'col', 'row'), parts along dimension 0, as said below
- right_sides: bfloat16 [10, 4096, 256], P('groups', 'row'), parts along dimension 0, may hold values from -6 to 6
Outputs:
- solution: bfloat16 [10, 4096, 256], P('groups', 'col', 'row'), parts along dimension 0
There are 2 independent parts, one for each index of `groups`. A program takes and returns all parts, laid end to end along the dimension named above; each array names one. Nothing has to cross between parts.
Inputs may be any that keep to these rules, and one draw needn't show every extreme that they name: `inverse_blocks`: each block is lower triangular with a diagonal of 0.5 to 2, hence invertible.
All inputs are finite; a program needn't handle non-finite values.
Results may differ from a plain program's by a relative error of at most 0.0095.
Values may be sent and summed in bfloat16 or wider, within the bound.
A program may use at most 64 MiB of HBM per device.

v0:
```python
import jax
import jax.numpy as jnp
from jax import lax
from jax.sharding import PartitionSpec as P


def pair_index(block_row, column_index):
    return block_row * (block_row - 1) // 2 + column_index


def per_device(factor_blocks, inverse_blocks, right_sides):
    steps_total = right_sides.shape[0]
    angles = right_sides.shape[2]
    col_rows = inverse_blocks.shape[1]
    solved = []
    outputs = []
    for block_row in range(steps_total):
        residual = right_sides[block_row].astype(jnp.float32)
        if block_row > 0:
            partial_value = jnp.zeros((right_sides.shape[1], angles), jnp.float32)
            for column_index in range(block_row):
                partial_value = partial_value + jnp.dot(
                    factor_blocks[pair_index(block_row, column_index)],
                    solved[column_index],
                    preferred_element_type=jnp.float32,
                )
            residual = residual - lax.psum(partial_value, "col")
        residual_bf = residual.astype(jnp.bfloat16)
        term = jnp.dot(inverse_blocks[block_row], residual_bf, preferred_element_type=jnp.float32)
        share = lax.psum_scatter(term, "row", scatter_dimension=1, tiled=True).astype(jnp.bfloat16)
        outputs.append(share)
        if block_row + 1 < steps_total:
            current = lax.all_gather(share, "row", axis=1, tiled=True)
        else:
            current = jnp.zeros((col_rows, angles), jnp.bfloat16)
        solved.append(current)
    return jnp.stack(outputs, axis=0)


def solution(mesh):
    placed = (P("groups", "row", "col"), P("groups", "col", "row"), P("groups", "row", None))
    return jax.shard_map(
        per_device, mesh=mesh, in_specs=placed, out_specs=P("groups", "col", "row"), check_vma=False
    )
```

profile of v0, /device:TPU:0, one launch (start us, length us, event | category | flops | bytes accessed | tf_op | source)
XLA Modules:
  0.0 406.6 jit_solution(15479284260959443623)
XLA Ops:
  6.5 3.4 fusion.28
  9.9 0.0 reduce-scatter.6.cloned.1.call-update
  10.0 0.0 all-reduce.5.cloned.1.call-start
  10.0 30.1 %reduce-scatter.6.cloned.1.call-done = f32[1024,64]{0,1:T(8,128)} async-done(((f32[1024,256]{0,1:T(8,128)}), f32[1024,64]{0,1:T(8,128)}) %reduce-scatter.6.cloned.1.call-update) | async-done | bytes 262160 | tf_op jit(solution)/shard_map/reduce_scatter | solution.py:30
  40.1 1.6 bitcast_dynamic-update-slice_fusion.4
  41.8 15.9 %all_gather.12 = bf16[1024,256]{0,1:T(8,128)(2,1)S(1)} all-gather(bf16[1024,64]{0,1:T(8,128)(2,1)S(1)} %get-tuple-element.12), channel_id=1, replica_groups=mesh['groups'=2,'row'=4,'col'=4] {'row'}, dimensions={1}, use_global_device_ids=true | all-gather | bytes 655360 | tf_op jit(solution)/shard_map/all_gather | solution.py:33
  57.7 3.5 fusion.45
  61.2 0.0 all-reduce.5.cloned.1.call-update
  61.2 0.0 reduce-scatter.8.cloned.1.call-start
  61.3 34.7 %all-reduce.5.cloned.1.call-done = f32[1024,256]{1,0:T(8,128)} async-done(((f32[1024,256]{1,0:T(8,128)}), f32[1024,256]{1,0:T(8,128)}) %all-reduce.5.cloned.1.call-update) | async-done | bytes 1048592 | tf_op jit(solution)/shard_map/psum | solution.py:27
  96.0 3.7 fusion.48
  99.7 0.0 reduce-scatter.8.cloned.1.call-update
  99.7 0.0 all-reduce.7.cloned.1.call-start
  99.8 27.9 %reduce-scatter.8.cloned.1.call-done = f32[1024,64]{0,1:T(8,128)} async-done(((f32[1024,256]{0,1:T(8,128)}), f32[1024,64]{0,1:T(8,128)}) %reduce-scatter.8.cloned.1.call-update) | async-done | bytes 262160 | tf_op jit(solution)/shard_map/reduce_scatter | solution.py:30
  127.6 1.6 bitcast_dynamic-update-slice_fusion.3
  129.3 16.0 %all_gather.13 = bf16[1024,256]{0,1:T(8,128)(2,1)S(1)} all-gather(bf16[1024,64]{0,1:T(8,128)(2,1)S(1)} %get-tuple-element.10), channel_id=1, replica_groups=mesh['groups'=2,'row'=4,'col'=4] {'row'}, dimensions={1}, use_global_device_ids=true | all-gather | bytes 655360 | tf_op jit(solution)/shard_map/all_gather | solution.py:33
  145.2 0.8 copy-done.4
  146.0 2.3 fusion.20
  148.4 3.3 fusion.63
  151.7 0.0 all-reduce.7.cloned.1.call-update
  151.7 0.0 reduce-scatter.10.cloned.1.call-start
  151.8 34.7 %all-reduce.7.cloned.1.call-done = f32[1024,256]{1,0:T(8,128)} async-done(((f32[1024,256]{1,0:T(8,128)}), f32[1024,256]{1,0:T(8,128)}) %all-reduce.7.cloned.1.call-update) | async-done | bytes 1048592 | tf_op jit(solution)/shard_map/psum | solution.py:27
  186.5 3.6 fusion.51
  190.1 0.0 reduce-scatter.10.cloned.1.call-update
  190.1 0.0 all-reduce.9.cloned.1.call-start
  190.2 3.5 fusion.14
  193.7 24.4 %reduce-scatter.10.cloned.1.call-done = f32[1024,64]{0,1:T(8,128)} async-done(((f32[1024,256]{0,1:T(8,128)}), f32[1024,64]{0,1:T(8,128)}) %reduce-scatter.10.cloned.1.call-update) | async-done | bytes 262160 | tf_op jit(solution)/shard_map/reduce_scatter | solution.py:30
  218.0 1.7 bitcast_dynamic-update-slice_fusion.2
  219.8 16.0 %all_gather.14 = bf16[1024,256]{0,1:T(8,128)(2,1)S(1)} all-gather(bf16[1024,64]{0,1:T(8,128)(2,1)S(1)} %get-tuple-element.8), channel_id=1, replica_groups=mesh['groups'=2,'row'=4,'col'=4] {'row'}, dimensions={1}, use_global_device_ids=true | all-gather | bytes 655360 | tf_op jit(solution)/shard_map/all_gather | solution.py:33
  235.7 0.8 copy-done.5
  236.5 2.3 fusion.12
  238.9 3.3 fusion.72
  242.2 0.0 reduce-scatter.12.cloned.1.call-start
  242.3 34.7 %all-reduce.9.cloned.1.call-done = f32[1024,256]{1,0:T(8,128)} async-done(((f32[1024,256]{1,0:T(8,128)}), f32[1024,256]{1,0:T(8,128)}) %all-reduce.9.cloned.1.call-update) | async-done | bytes 1048592 | tf_op jit(solution)/shard_map/psum | solution.py:27
  277.0 3.6 fusion.54
  280.6 0.0 all-reduce.11.cloned.1.call-start
  280.7 3.6 fusion.6
  284.3 3.3 fusion.4
  287.6 21.0 %reduce-scatter.12.cloned.1.call-done = f32[1024,64]{0,1:T(8,128)} async-done(((f32[1024,256]{0,1:T(8,128)}), f32[1024,64]{0,1:T(8,128)}) %reduce-scatter.12.cloned.1.call-update) | async-done | bytes 262160 | tf_op jit(solution)/shard_map/reduce_scatter | solution.py:30
  308.6 1.8 bitcast_dynamic-update-slice_fusion.1
  310.3 15.9 %all_gather.15 = bf16[1024,256]{0,1:T(8,128)(2,1)S(1)} all-gather(bf16[1024,64]{0,1:T(8,128)(2,1)S(1)} %get-tuple-element.6), channel_id=1, replica_groups=mesh['groups'=2,'row'=4,'col'=4] {'row'}, dimensions={1}, use_global_device_ids=true | all-gather | bytes 655360 | tf_op jit(solution)/shard_map/all_gather | solution.py:33
  326.2 2.3 fusion.2
  328.6 3.4 fusion.84
  332.0 0.0 reduce-scatter.14.cloned.1.call-start
  332.1 34.8 %all-reduce.11.cloned.1.call-done = f32[1024,256]{1,0:T(8,128)} async-done(((f32[1024,256]{1,0:T(8,128)}), f32[1024,256]{1,0:T(8,128)}) %all-reduce.11.cloned.1.call-update) | async-done | bytes 1048592 | tf_op jit(solution)/shard_map/psum | solution.py:27
  366.8 3.7 fusion.57
  370.5 27.9 %reduce-scatter.14.cloned.1.call-done = f32[1024,64]{0,1:T(8,128)} async-done(((f32[1024,256]{0,1:T(8,128)}), f32[1024,64]{0,1:T(8,128)}) %reduce-scatter.14.cloned.1.call-update) | async-done | bytes 262160 | tf_op jit(solution)/shard_map/reduce_scatter | solution.py:30
  398.4 1.6 bitcast_dynamic-update-slice_fusion
  (17 shorter events, 0.1 us)
Async XLA Ops:
  6.5 33.6 %reduce-scatter.6.cloned.1.call-start = ((), (), s32[]{:S(2)}) async-start(), calls=%async_computation.5 | async-start | bytes 1310720 | tf_op jit(solution)/shard_map/reduce_scatter | solution.py:30
  10.0 86.0 %all-reduce.5.cloned.1.call-start = ((), (), s32[]{:S(2)}) async-start(), calls=%async_computation.6 | async-start | bytes 2097152 | tf_op jit(solution)/shard_map/psum | solution.py:27
  57.7 38.3 %copy-start = (bf16[5,1024,256]{2,1,0:T(8,128)(2,1)S(1)}, bf16[5,1024,256]{2,1,0:T(8,128)(2,1)}, u32[]{:S(2)}) copy-start(bf16[5,1024,256]{2,1,0:T(8,128)(2,1)} %param.5) | copy-start | bytes 7864324
  61.2 66.4 %reduce-scatter.8.cloned.1.call-start = ((), (), s32[]{:S(2)}) async-start(), calls=%async_computation.7 | async-start | bytes 1310720 | tf_op jit(solution)/shard_map/reduce_scatter | solution.py:30
  99.7 86.7 %all-reduce.7.cloned.1.call-start = ((), (), s32[]{:S(2)}) async-start(), calls=%async_computation.8 | async-start | bytes 2097152 | tf_op jit(solution)/shard_map/psum | solution.py:27
  145.2 0.8 copy-start.4
  151.7 66.3 %reduce-scatter.10.cloned.1.call-start = ((), (), s32[]{:S(2)}) async-start(), calls=%async_computation.9 | async-start | bytes 1310720 | tf_op jit(solution)/shard_map/reduce_scatter | solution.py:30
  190.1 86.8 %all-reduce.9.cloned.1.call-start = ((), (), s32[]{:S(2)}) async-start(), calls=%async_computation.10 | async-start | bytes 2097152 | tf_op jit(solution)/shard_map/psum | solution.py:27
  218.0 20.8 %copy-start.3 = (f32[256,1024]{0,1:T(8,128)S(1)}, f32[256,1024]{0,1:T(8,128)}, u32[]{:S(2)}) copy-start(f32[256,1024]{0,1:T(8,128)} %fusion.14) | copy-start | bytes 3145732
  235.7 0.8 copy-start.5
  242.2 66.3 %reduce-scatter.12.cloned.1.call-start = ((), (), s32[]{:S(2)}) async-start(), calls=%async_computation.11 | async-start | bytes 1310720 | tf_op jit(solution)/shard_map/reduce_scatter | solution.py:30
  280.6 86.2 %all-reduce.11.cloned.1.call-start = ((), (), s32[]{:S(2)}) async-start(), calls=%async_computation.12 | async-start | bytes 2097152 | tf_op jit(solution)/shard_map/psum | solution.py:27
  280.7 3.6 copy-start.6
  308.6 20.0 %copy-start.1 = (f32[256,1024]{0,1:T(8,128)S(1)}, f32[256,1024]{0,1:T(8,128)}, u32[]{:S(2)}) copy-start(f32[256,1024]{0,1:T(8,128)} %fusion.6) | copy-start | bytes 3145732
  308.6 20.0 %copy-start.2 = (f32[256,1024]{0,1:T(8,128)S(1)}, f32[256,1024]{0,1:T(8,128)}, u32[]{:S(2)}) copy-start(f32[256,1024]{0,1:T(8,128)} %fusion.4) | copy-start | bytes 3145732
  332.0 66.4 %reduce-scatter.14.cloned.1.call-start = ((), (), s32[]{:S(2)}) async-start(), calls=%async_computation.13 | async-start | bytes 1310720 | tf_op jit(solution)/shard_map/reduce_scatter | solution.py:30
Sparse Core Ops, SparseCore 0:
  10.1 29.9 reduce-scatter.5
  61.3 34.6 all-reduce.4
  99.8 27.7 reduce-scatter.7
  151.8 34.5 all-reduce.6
  190.2 27.7 reduce-scatter.9
  242.3 34.5 all-reduce.8
  280.8 27.7 reduce-scatter.11
  332.1 34.6 all-reduce.10
  370.6 27.7 reduce-scatter.13
where the time goes:
time: 407 us
  waiting for transfers between devices  270 us (66%)
  blocking collectives  63.8 us (16%)
  matrix products  49 us (12%)
  between operations  13.3 us (3%)
  other arithmetic  8.36 us (2%)
    psum x4, waiting for transfers between devices, per_device(): residual = residual - lax.psum(partial_value, 'col')  139 us
    reduce_scatter x5, waiting for transfers between devices, per_device(): lax.psum_scatter(term, 'row', scatter_dimension=1, tiled=True)  131 us
    all_gather x4, blocking collectives, per_device(): current = lax.all_gather(share, 'row', axis=1, tiled=True)  63.8 us
    dot_general x10, matrix products, per_device(): jnp.dot(factor_blocks[pair_index(block_row, column_index)], solved[column...  30.9 us
    dot_general x5, matrix products, per_device(): jnp.dot(inverse_blocks[block_row], residual_bf, preferred_element_type=jn...  18.1 us
  transfers between devices with their start and end apart: 9, of which 9 were waited for; matrix products, arithmetic and copies ran while one was open for 3% of the time, Pallas kernels for 0%

commit v1 on v0

--- a/solution.py
+++ b/solution.py
@@ -24,7 +24,7 @@
                     solved[column_index],
                     preferred_element_type=jnp.float32,
                 )
-            residual = residual - lax.psum(partial_value, "col")
+            residual = residual - jnp.sum(jax.lax.all_gather(partial_value, "col"), axis=0)
         residual_bf = residual.astype(jnp.bfloat16)
         term = jnp.dot(inverse_blocks[block_row], residual_bf, preferred_element_type=jnp.float32)
         share = lax.psum_scatter(term, "row", scatter_dimension=1, tiled=True).astype(jnp.bfloat16)

time: 407 us -> 440 us (1.081)
  local copies, waits for them, and re-layouts: 1.62 us -> 28.4 us
  other arithmetic: 8.36 us -> 27.2 us
  waiting for transfers between devices: 270 us -> 260 us
    psum x4 -> x0, waiting for transfers between devices: 139 us -> none  [per_device(): residual = residual - lax.psum(partial_value, 'col')]
    all_gather x0 -> x4, waiting for transfers between devices: none -> 128 us  [per_device(): jax.lax.all_gather(partial_value, 'col')]
    all_gather x0 -> x4, local copies, waits for them, and re-layouts: none -> 24.2 us  [per_device(): jax.lax.all_gather(partial_value, 'col')]
    reduce_sum x0 -> x4, other arithmetic: none -> 19 us  [per_device(): jnp.sum(jax.lax.all_gather(partial_value, 'col'), axis=0)]
where the time goes in v1:
time: 440 us; the launch traced here: 439 us
  waiting for transfers between devices  260 us (59%)
  blocking collectives  63.8 us (14%)
  matrix products  45.5 us (10%)
  local copies, waits for them, and re-layouts  28.4 us (6%)
  other arithmetic  27.2 us (6%)
  between operations  13.3 us (3%)
    reduce_scatter x5, waiting for transfers between devices, per_device(): lax.psum_scatter(term, 'row', scatter_dimension=1, tiled=True)  131 us
    all_gather x4, waiting for transfers between devices, per_device(): jax.lax.all_gather(partial_value, 'col')  128 us
    all_gather x4, blocking collectives, per_device(): current = lax.all_gather(share, 'row', axis=1, tiled=True)  63.8 us
    dot_general x10, matrix products, per_device(): jnp.dot(factor_blocks[pair_index(block_row, column_index)], solved[column...  28.8 us
    all_gather x4, local copies, waits for them, and re-layouts, per_device(): jax.lax.all_gather(partial_value, 'col')  24.2 us
    reduce_sum x4, other arithmetic, per_device(): jnp.sum(jax.lax.all_gather(partial_value, 'col'), axis=0)  19 us
    dot_general x5, matrix products, per_device(): jnp.dot(inverse_blocks[block_row], residual_bf, preferred_element_type=jn...  16.7 us
  transfers between devices with their start and end apart: 9, of which 9 were waited for; matrix products, arithmetic and copies ran while one was open for 3% of the time, Pallas kernels for 0%

profile of v1, /device:TPU:0, one launch (start us, length us, event | category | flops | bytes accessed | tf_op | source)
XLA Modules:
  0.0 438.5 jit_solution(7066276382499517516)
XLA Ops:
  6.5 3.4 fusion.28
  10.0 30.1 %reduce-scatter.6.cloned.1.call-done = f32[1024,64]{0,1:T(8,128)} async-done(((f32[1024,256]{0,1:T(8,128)}), f32[1024,64]{0,1:T(8,128)}) %reduce-scatter.6.cloned.1.call-update) | async-done | bytes 262160 | tf_op jit(solution)/shard_map/reduce_scatter | solution.py:30
  40.1 1.6 bitcast_dynamic-update-slice_fusion.4
  41.7 16.0 %all_gather.36 = bf16[1024,256]{0,1:T(8,128)(2,1)S(1)} all-gather(bf16[1024,64]{0,1:T(8,128)(2,1)S(1)} %get-tuple-element.12), channel_id=1, replica_groups=mesh['groups'=2,'row'=4,'col'=4] {'row'}, dimensions={1}, use_global_device_ids=true | all-gather | bytes 655360 | tf_op jit(solution)/shard_map/all_gather | solution.py:33
  57.7 3.3 fusion.45
  61.1 2.5 fusion.101
  63.8 30.2 %all-gather.9.cloned.1.call-done = f32[4096,256]{0,1:T(8,128)} async-done(((f32[1024,256]{0,1:T(8,128)}), f32[4096,256]{0,1:T(8,128)}) %all-gather.9.cloned.1.call-update) | async-done | bytes 4194320 | tf_op jit(solution)/shard_map/all_gather | solution.py:27
  94.0 6.1 %reshape.8 = f32[4,1024,256]{1,0,2:T(4,128)} reshape(f32[4096,256]{0,1:T(8,128)} %all-gather.9.cloned.1.call-done) | data formatting | bytes 8388608 | tf_op jit(solution)/shard_map/all_gather | solution.py:27
  100.0 4.7 %reduce_sum.44 = f32[1024,256]{0,1:T(8,128)S(1)} reduce(f32[4,1024,256]{1,0,2:T(4,128)} %reshape.8, f32[]{:T(128)} %constant.0.clone.1), dimensions={0}, to_apply=%region_1.0 | reduce | flops 786432 | bytes 5242884 | tf_op jit(solution)/shard_map/reduce_sum | solution.py:27
  104.8 3.3 fusion.48
  108.2 27.4 %reduce-scatter.8.cloned.1.call-done = f32[1024,64]{0,1:T(8,128)} async-done(((f32[1024,256]{0,1:T(8,128)}), f32[1024,64]{0,1:T(8,128)}) %reduce-scatter.8.cloned.1.call-update) | async-done | bytes 262160 | tf_op jit(solution)/shard_map/reduce_scatter | solution.py:30
  135.6 1.6 bitcast_dynamic-update-slice_fusion.3
  137.2 16.0 %all_gather.39 = bf16[1024,256]{0,1:T(8,128)(2,1)S(1)} all-gather(bf16[1024,64]{0,1:T(8,128)(2,1)S(1)} %get-tuple-element.10), channel_id=1, replica_groups=mesh['groups'=2,'row'=4,'col'=4] {'row'}, dimensions={1}, use_global_device_ids=true | all-gather | bytes 655360 | tf_op jit(solution)/shard_map/all_gather | solution.py:33
  153.2 0.8 copy-done.2
  154.0 2.4 fusion.20
  156.4 3.3 fusion.63
  159.7 0.2 reduce-scatter.10.cloned.1.call-start
  159.9 0.2 copy.9
  160.2 32.5 %all-gather.11.cloned.1.call-done = f32[4096,256]{0,1:T(8,128)} async-done(((f32[1024,256]{0,1:T(8,128)}), f32[4096,256]{0,1:T(8,128)}) %all-gather.11.cloned.1.call-update) | async-done | bytes 4194320 | tf_op jit(solution)/shard_map/all_gather | solution.py:27
  192.7 6.1 %reshape.9 = f32[4,1024,256]{1,0,2:T(4,128)} reshape(f32[4096,256]{0,1:T(8,128)} %all-gather.11.cloned.1.call-done) | data formatting | bytes 8388608 | tf_op jit(solution)/shard_map/all_gather | solution.py:27
  198.7 4.7 %reduce_sum.46 = f32[1024,256]{0,1:T(8,128)S(1)} reduce(f32[4,1024,256]{1,0,2:T(4,128)} %reshape.9, f32[]{:T(128)} %constant.0.clone.1), dimensions={0}, to_apply=%region_3.0 | reduce | flops 786432 | bytes 5242884 | tf_op jit(solution)/shard_map/reduce_sum | solution.py:27
  203.5 3.3 fusion.51
  206.9 2.5 fusion.14
  209.4 24.9 %reduce-scatter.10.cloned.1.call-done = f32[1024,64]{0,1:T(8,128)} async-done(((f32[1024,256]{0,1:T(8,128)}), f32[1024,64]{0,1:T(8,128)}) %reduce-scatter.10.cloned.1.call-update) | async-done | bytes 262160 | tf_op jit(solution)/shard_map/reduce_scatter | solution.py:30
  234.3 1.6 bitcast_dynamic-update-slice_fusion.2
  235.9 16.0 %all_gather.42 = bf16[1024,256]{0,1:T(8,128)(2,1)S(1)} all-gather(bf16[1024,64]{0,1:T(8,128)(2,1)S(1)} %get-tuple-element.8), channel_id=1, replica_groups=mesh['groups'=2,'row'=4,'col'=4] {'row'}, dimensions={1}, use_global_device_ids=true | all-gather | bytes 655360 | tf_op jit(solution)/shard_map/all_gather | solution.py:33
  251.9 2.5 fusion.12
  254.4 3.3 fusion.72
  257.8 0.2 copy.10
  258.0 32.7 %all-gather.13.cloned.1.call-done = f32[4096,256]{0,1:T(8,128)} async-done(((f32[1024,256]{0,1:T(8,128)}), f32[4096,256]{0,1:T(8,128)}) %all-gather.13.cloned.1.call-update) | async-done | bytes 4194320 | tf_op jit(solution)/shard_map/all_gather | solution.py:27
  290.7 6.1 %reshape.10 = f32[4,1024,256]{1,0,2:T(4,128)} reshape(f32[4096,256]{0,1:T(8,128)} %all-gather.13.cloned.1.call-done) | data formatting | bytes 8388608 | tf_op jit(solution)/shard_map/all_gather | solution.py:27
  296.8 4.7 %reduce_sum.48 = f32[1024,256]{0,1:T(8,128)S(1)} reduce(f32[4,1024,256]{1,0,2:T(4,128)} %reshape.10, f32[]{:T(128)} %constant.0.clone.1), dimensions={0}, to_apply=%region_5.0 | reduce | flops 786432 | bytes 5242884 | tf_op jit(solution)/shard_map/reduce_sum | solution.py:27
  301.5 3.4 fusion.54
  304.9 0.3 all-gather.15.cloned.1.call-start
  305.2 2.3 fusion.6
  307.6 3.3 fusion.4
  310.9 21.5 %reduce-scatter.12.cloned.1.call-done = f32[1024,64]{0,1:T(8,128)} async-done(((f32[1024,256]{0,1:T(8,128)}), f32[1024,64]{0,1:T(8,128)}) %reduce-scatter.12.cloned.1.call-update) | async-done | bytes 262160 | tf_op jit(solution)/shard_map/reduce_scatter | solution.py:30
  332.4 1.7 bitcast_dynamic-update-slice_fusion.1
  334.1 16.0 %all_gather.45 = bf16[1024,256]{0,1:T(8,128)(2,1)S(1)} all-gather(bf16[1024,64]{0,1:T(8,128)(2,1)S(1)} %get-tuple-element.6), channel_id=1, replica_groups=mesh['groups'=2,'row'=4,'col'=4] {'row'}, dimensions={1}, use_global_device_ids=true | all-gather | bytes 655360 | tf_op jit(solution)/shard_map/all_gather | solution.py:33
  350.1 2.3 fusion.2
  352.4 3.4 fusion.84
  355.9 0.2 copy.11
  356.1 32.7 %all-gather.15.cloned.1.call-done = f32[4096,256]{0,1:T(8,128)} async-done(((f32[1024,256]{0,1:T(8,128)}), f32[4096,256]{0,1:T(8,128)}) %all-gather.15.cloned.1.call-update) | async-done | bytes 4194320 | tf_op jit(solution)/shard_map/all_gather | solution.py:27
  388.8 6.1 %reshape.11 = f32[4,1024,256]{1,0,2:T(4,128)} reshape(f32[4096,256]{0,1:T(8,128)} %all-gather.15.cloned.1.call-done) | data formatting | bytes 8388608 | tf_op jit(solution)/shard_map/all_gather | solution.py:27
  394.8 4.7 %reduce_sum.50 = f32[1024,256]{0,1:T(8,128)S(1)} reduce(f32[4,1024,256]{1,0,2:T(4,128)} %reshape.11, f32[]{:T(128)} %constant.0.clone.1), dimensions={0}, to_apply=%region_7.0 | reduce | flops 786432 | bytes 5242884 | tf_op jit(solution)/shard_map/reduce_sum | solution.py:27
  399.6 3.3 fusion.57
  402.9 27.4 %reduce-scatter.14.cloned.1.call-done = f32[1024,64]{0,1:T(8,128)} async-done(((f32[1024,256]{0,1:T(8,128)}), f32[1024,64]{0,1:T(8,128)}) %reduce-scatter.14.cloned.1.call-update) | async-done | bytes 262160 | tf_op jit(solution)/shard_map/reduce_scatter | solution.py:30
  430.4 1.6 bitcast_dynamic-update-slice_fusion
  (28 shorter events, 0.6 us)
Async XLA Ops:
  6.5 33.6 %reduce-scatter.6.cloned.1.call-start = ((), (), s32[]{:S(2)}) async-start(), calls=%async_computation.5 | async-start | bytes 1310720 | tf_op jit(solution)/shard_map/reduce_scatter | solution.py:30
  10.0 84.0 %all-gather.9.cloned.1.call-start = ((), (), s32[]{:S(2)}) async-start(), calls=%async_computation.10 | async-start | bytes 5242880 | tf_op jit(solution)/shard_map/all_gather | solution.py:27
  61.0 74.5 %reduce-scatter.8.cloned.1.call-start = ((), (), s32[]{:S(2)}) async-start(), calls=%async_computation.6 | async-start | bytes 1310720 | tf_op jit(solution)/shard_map/reduce_scatter | solution.py:30
  108.1 84.6 %all-gather.11.cloned.1.call-start = ((), (), s32[]{:S(2)}) async-start(), calls=%async_computation.11 | async-start | bytes 5242880 | tf_op jit(solution)/shard_map/all_gather | solution.py:27
  153.2 0.8 copy-start.2
  154.0 6.0 %copy-start = (bf16[1,1024,256]{2,1,0:T(8,128)(2,1)S(1)}, bf16[1,1024,256]{2,1,0:T(8,128)(2,1)}, u32[]{:S(2)}) copy-start(bf16[1,1024,256]{2,1,0:T(8,128)(2,1)} %get-tuple-element.15) | copy-start | bytes 1572868
  159.7 74.6 %reduce-scatter.10.cloned.1.call-start = ((), (), s32[]{:S(2)}) async-start(), calls=%async_computation.7 | async-start | bytes 1310720 | tf_op jit(solution)/shard_map/reduce_scatter | solution.py:30
  206.8 83.9 %all-gather.13.cloned.1.call-start = ((), (), s32[]{:S(2)}) async-start(), calls=%async_computation.12 | async-start | bytes 5242880 | tf_op jit(solution)/shard_map/all_gather | solution.py:27
  251.9 5.9 %copy-start.4 = (bf16[1024,256]{0,1:T(8,128)(2,1)}, bf16[1024,256]{0,1:T(8,128)(2,1)S(1)}, u32[]{:S(2)}) copy-start(bf16[1024,256]{0,1:T(8,128)(2,1)S(1)} %all_gather.42) | copy-start | bytes 1572868
  257.8 74.7 %reduce-scatter.12.cloned.1.call-start = ((), (), s32[]{:S(2)}) async-start(), calls=%async_computation.8 | async-start | bytes 1310720 | tf_op jit(solution)/shard_map/reduce_scatter | solution.py:30
  301.5 3.7 copy-start.3
  304.9 2.6 copy-start.5
  304.9 83.9 %all-gather.15.cloned.1.call-start = ((), (), s32[]{:S(2)}) async-start(), calls=%async_computation.13 | async-start | bytes 5242880 | tf_op jit(solution)/shard_map/all_gather | solution.py:27
  332.4 20.0 %copy-start.1 = (f32[256,1024]{1,0:T(8,128)S(1)}, f32[256,1024]{1,0:T(8,128)}, u32[]{:S(2)}) copy-start(f32[256,1024]{1,0:T(8,128)} %fusion.4) | copy-start | bytes 3145732
  355.9 74.5 %reduce-scatter.14.cloned.1.call-start = ((), (), s32[]{:S(2)}) async-start(), calls=%async_computation.9 | async-start | bytes 1310720 | tf_op jit(solution)/shard_map/reduce_scatter | solution.py:30
Sparse Core Ops, SparseCore 0:
  10.1 29.9 reduce-scatter.5
  61.2 32.7 all-gather.8
  108.2 27.2 reduce-scatter.7
  159.8 32.8 all-gather.10
  206.9 27.2 reduce-scatter.9
  257.9 32.8 all-gather.12
  305.1 27.3 reduce-scatter.11
  356.0 32.7 all-gather.14
  403.0 27.2 reduce-scatter.13
